TPU v7x, 32 devices: a whole 2x2x4 slice. The times are simulated.
32 devices in a mesh: seq: 8 (over y, x, core), head: 4 (over z).
Axes of the slice: x: 2, y: 2, z: 4, core: 2. Of those that a mesh axis runs over, the one named last changes fastest.
Arguments:
- projected: bfloat16 [4096, 3, 3072], P(('seq', 'head')), may hold values from -70 to 70
- key_lists: int32 [48, 32, 8], P('head', 'seq'), may hold values from 0 to 31, as said below
- list_counts: int32 [48, 32], P('head', 'seq'), may hold values from 1 to 8
Outputs:
- attended: bfloat16 [4096, 3072], P(('seq', 'head'))
Inputs may be any that keep to these rules, and one draw needn't show every extreme that they name: `key_lists`: entries are key block numbers; no list names its own query block, and the entries of one list are distinct. Entry j of the list of query block b in head h lies on seq shard (b // 4 + o + j) mod 8, o depending on h and b. Over the 12 heads of one head group and the query blocks of one seq shard, exactly 48 entries lie on each seq shard, entries past a list's count included, and the entries that lie on one seq shard name at most two distinct key blocks: at most one whose number within its shard is below 2 and at most one whose number is at least that. In every draw some head group, seq shard and owning seq shard have two.
All inputs are finite; a program needn't handle non-finite values.
Results may differ from a plain program's by a relative error of at most 0.005.
Values may be sent and summed in bfloat16 or wider, within the bound.
No kernel may reach another device: no remote copies, remote signals or barrier semaphores. Data moves between devices by JAX's collectives and lax.ppermute only.
A program may use at most 128 MiB of HBM per device.

v0:
```python
import math
import jax
import jax.numpy as jnp
from jax import lax
from jax.sharding import PartitionSpec as P

NEG_FILL = -1e30


def attend_rows(query_part, gathered, live_cols, head_size):
    row_count, seen_blocks, block_len, doubled = gathered.shape
    key_rows = gathered[..., :head_size].reshape(row_count, seen_blocks * block_len, head_size)
    value_rows = gathered[..., head_size:].reshape(row_count, seen_blocks * block_len, head_size)
    attention_scores = jnp.einsum(
        "rqd,rkd->rqk", query_part, key_rows, preferred_element_type=jnp.float32
    ) * (1.0 / math.sqrt(head_size))
    attention_scores = attention_scores.reshape(row_count, block_len, seen_blocks, block_len)
    attention_scores = jnp.where(live_cols[:, None, :, None], attention_scores, NEG_FILL)
    row_top = jnp.max(attention_scores, axis=(2, 3), keepdims=True)
    exp_scores = jnp.exp(attention_scores - row_top)
    attention_weights = (exp_scores / jnp.sum(exp_scores, axis=(2, 3), keepdims=True)).astype(
        jnp.bfloat16
    )
    attention_weights = attention_weights.reshape(row_count, block_len, seen_blocks * block_len)
    return jnp.einsum(
        "rqk,rkd->rqd", attention_weights, value_rows, preferred_element_type=jnp.float32
    )


def on_device(projected, key_lists, list_counts):
    seq_count = lax.axis_size("seq")
    heads_dev, blocks_dev, list_most = key_lists.shape
    regrouped = lax.all_to_all(projected, "head", split_axis=2, concat_axis=0, tiled=True)
    block_len = regrouped.shape[0] // blocks_dev
    group_width = regrouped.shape[2]
    head_size = group_width // heads_dev
    row_count = heads_dev * blocks_dev
    splitted = regrouped.reshape(blocks_dev, block_len, 3, heads_dev, head_size)
    queries = splitted[:, :, 0].transpose(2, 0, 1, 3).reshape(row_count, block_len, head_size)
    kv_pairs = jnp.concatenate([splitted[:, :, 1], splitted[:, :, 2]], axis=-1)
    kv_pairs = kv_pairs.transpose(2, 0, 1, 3).reshape(row_count, block_len, 2 * head_size)
    entries = key_lists.reshape(row_count * list_most)
    owners = entries // blocks_dev
    row_head = jnp.arange(row_count * list_most, dtype=jnp.int32) // (blocks_dev * list_most)
    capacity = row_count * list_most // seq_count
    wanted = row_head * blocks_dev + entries % blocks_dev
    onehot = (owners[:, None] == jnp.arange(seq_count, dtype=jnp.int32)[None, :]).astype(jnp.int32)
    within = jnp.sum(onehot * (jnp.cumsum(onehot, axis=0) - 1), axis=1)
    slot_ids = owners * capacity + within
    request = (
        jnp.zeros((seq_count * capacity,), jnp.int32)
        .at[slot_ids]
        .set(wanted)
        .reshape(seq_count, capacity)
    )
    asked_for = lax.all_to_all(request, "seq", split_axis=0, concat_axis=0, tiled=True)
    served = jnp.take(kv_pairs, asked_for.reshape(-1), axis=0).reshape(
        seq_count, capacity, block_len, 2 * head_size
    )
    fetched = lax.all_to_all(served, "seq", split_axis=0, concat_axis=0, tiled=True)
    fetched = fetched.reshape(seq_count * capacity, block_len, 2 * head_size)
    entry_slots = slot_ids.reshape(row_count, list_most)
    row_counts = list_counts.reshape(row_count)
    group_rows = 4

    def one_group(group_index):
        start = group_index * group_rows
        query_part = lax.dynamic_slice_in_dim(queries, start, group_rows, 0)
        own_pairs = lax.dynamic_slice_in_dim(kv_pairs, start, group_rows, 0)
        slot_part = lax.dynamic_slice_in_dim(entry_slots, start, group_rows, 0)
        count_part = lax.dynamic_slice_in_dim(row_counts, start, group_rows, 0)
        listed = jnp.take(fetched, slot_part.reshape(-1), axis=0).reshape(
            group_rows, list_most, block_len, 2 * head_size
        )
        gathered = jnp.concatenate([own_pairs[:, None], listed], axis=1)
        live_cols = jnp.concatenate(
            [
                jnp.ones((group_rows, 1), bool),
                jnp.arange(list_most, dtype=jnp.int32)[None, :] < count_part[:, None],
            ],
            axis=1,
        )
        return attend_rows(query_part, gathered, live_cols, head_size).astype(jnp.bfloat16)

    attended = lax.map(one_group, jnp.arange(row_count // group_rows, dtype=jnp.int32))
    attended = attended.reshape(row_count, block_len, head_size)
    laid_out = attended.reshape(heads_dev, blocks_dev * block_len, head_size).transpose(1, 0, 2)
    laid_out = laid_out.reshape(blocks_dev * block_len, group_width)
    return lax.all_to_all(laid_out, "head", split_axis=0, concat_axis=1, tiled=True)


def solution(mesh):
    return jax.shard_map(
        on_device,
        mesh=mesh,
        in_specs=(P(("seq", "head"), None, None), P("head", "seq", None), P("head", "seq")),
        out_specs=P(("seq", "head"), None),
        check_vma=False,
    )
```

profile of v0, /device:TPU:2, one launch (start us, length us, event | category | flops | bytes accessed | tf_op | source)
XLA Modules:
  0.0 542.2 jit_solution(7548757384802746488)
XLA Ops:
  2.4 2.9 scatter_custom_fusion
  6.0 4.3 all-to-all-start.1
  10.3 5.7 %copy.35 = bf16[128,3,3072]{0,1,2:T(4,128)(2,1)} copy(bf16[128,3,3072]{2,0,1:T(8,128)(2,1)} %param.5) | data formatting | bytes 4718592 | tf_op args[0]
  16.0 4.9 all-to-all-start
  22.1 69.7 %all-to-all-done = bf16[128,3,3072]{0,1,2:T(4,128)(2,1)S(1)} async-done(((bf16[128,3,3072]{0,1,2:T(4,128)(2,1)}), bf16[128,3,3072]{0,1,2:T(4,128)(2,1)S(1)}, u32[]{:S(2)}, u32[]{:S(2)}) %all-to-all-start) | async-done | bytes 2359328 | tf_op jit(solution)/shard_map/all_to_all | solution.py:33
  94.5 11.3 %gather_fusion.1 = bf16[384,128,128]{2,1,0:T(8,128)(2,1)} fusion(bf16[48,128,128]{2,1,0:T(8,128)(2,1)S(1)} %bitcast.78, s32[1024]{0:T(1024)S(1)} %pad_clamp_fusion.1), kind=kCustom, calls=%fused_computation.1 | custom fusion | bytes 25167360 | tf_op jit(solution)/shard_map/jit(_take)/gather | solution.py:57
  105.8 10.8 %broadcast_select_fusion.1 = bf16[8,48,128,128]{3,2,1,0:T(8,128)(2,1)} fusion(bf16[8,48,128,128]{3,2,1,0:T(8,128)(2,1)} %bitcast.81, pred[8,48]{1,0:T(8,128)(4,1)S(1)} %compare_and_fusion.1), kind=kLoop, calls=%fused_computation.39 | loop fusion | flops 6291456 | bytes 25166208 | tf_op jit(solution)/shard_map/jit(_take)/select_n | solution.py:57
  116.6 5.7 %all-to-all-start.2 = ((bf16[8,48,128,128]{3,2,1,0:T(8,128)(2,1)}), bf16[8,48,128,128]{3,2,1,0:T(8,128)(2,1)}, u32[]{:S(2)}, u32[]{:S(2)}) async-start(bf16[8,48,128,128]{3,2,1,0:T(8,128)(2,1)} %broadcast_select_fusion.1), calls=%async_computation.2 | async-start | bytes 25165824 | tf_op jit(solution)/shard_map/all_to_all | solution.py:60
  123.6 136.3 %all-to-all-done.2 = bf16[8,48,128,128]{3,2,1,0:T(8,128)(2,1)} async-done(((bf16[8,48,128,128]{3,2,1,0:T(8,128)(2,1)}), bf16[8,48,128,128]{3,2,1,0:T(8,128)(2,1)}, u32[]{:S(2)}, u32[]{:S(2)}) %all-to-all-start.2) | async-done | bytes 12582944 | tf_op jit(solution)/shard_map/all_to_all | solution.py:60
  259.9 256.2 %while.10 = (s32[]{:T(128)}, bf16[12,4,128,64]{2,1,3,0:T(4,128)(2,1)}, s32[12]{0:T(128)S(1)}, s32[48]{0:T(128)S(1)}, bf16[48,128,64]{1,2,0:T(8,128)(2,1)}, /*ind...) while((s32[]{:T(128)}, ...), condition=%wide.region_7.8_spmd, body=%wide.region_4.7_spmd.sunk | while | flops 234721344 | bytes 13664708 | solution.py:85
  261.2 6.3 %gather_fusion = bf16[32,128,128]{2,1,0:T(8,128)(2,1)} fusion(bf16[384,128,128]{2,1,0:T(8,128)(2,1)} %get-tuple-element.162, s32[1024]{0:T(1024)S(1)} %pad_clamp_fusion.3), kind=kCustom, calls=%fused_computation.clone.1 | custom fusion | bytes 2097280 | tf_op jit(solution)/shard_map/while/body/eval_jaxpr/jit(_take)/gather | solution.py:72
  267.6 1.7 copy.62
  270.6 3.0 fusion.71
  275.4 1.8 fusion.72
  278.4 2.2 fusion.73
  282.6 6.3 %gather_fusion = bf16[32,128,128]{2,1,0:T(8,128)(2,1)} fusion(bf16[384,128,128]{2,1,0:T(8,128)(2,1)} %get-tuple-element.162, s32[1024]{0:T(1024)S(1)} %pad_clamp_fusion.3), kind=kCustom, calls=%fused_computation.clone.1 | custom fusion | bytes 2097280 | tf_op jit(solution)/shard_map/while/body/eval_jaxpr/jit(_take)/gather | solution.py:72
  288.9 1.7 copy.62
  292.0 3.0 fusion.71
  296.8 1.8 fusion.72
  299.7 2.2 fusion.73
  303.9 6.3 %gather_fusion = bf16[32,128,128]{2,1,0:T(8,128)(2,1)} fusion(bf16[384,128,128]{2,1,0:T(8,128)(2,1)} %get-tuple-element.162, s32[1024]{0:T(1024)S(1)} %pad_clamp_fusion.3), kind=kCustom, calls=%fused_computation.clone.1 | custom fusion | bytes 2097280 | tf_op jit(solution)/shard_map/while/body/eval_jaxpr/jit(_take)/gather | solution.py:72
  310.2 1.7 copy.62
  313.3 3.0 fusion.71
  318.1 1.8 fusion.72
  321.1 2.2 fusion.73
  325.3 6.3 %gather_fusion = bf16[32,128,128]{2,1,0:T(8,128)(2,1)} fusion(bf16[384,128,128]{2,1,0:T(8,128)(2,1)} %get-tuple-element.162, s32[1024]{0:T(1024)S(1)} %pad_clamp_fusion.3), kind=kCustom, calls=%fused_computation.clone.1 | custom fusion | bytes 2097280 | tf_op jit(solution)/shard_map/while/body/eval_jaxpr/jit(_take)/gather | solution.py:72
  334.7 3.0 fusion.71
  339.5 1.8 fusion.72
  342.4 2.2 fusion.73
  346.6 6.3 %gather_fusion = bf16[32,128,128]{2,1,0:T(8,128)(2,1)} fusion(bf16[384,128,128]{2,1,0:T(8,128)(2,1)} %get-tuple-element.162, s32[1024]{0:T(1024)S(1)} %pad_clamp_fusion.3), kind=kCustom, calls=%fused_computation.clone.1 | custom fusion | bytes 2097280 | tf_op jit(solution)/shard_map/while/body/eval_jaxpr/jit(_take)/gather | solution.py:72
  352.9 1.7 copy.62
  356.0 3.0 fusion.71
  360.8 1.8 fusion.72
  363.8 2.2 fusion.73
  368.0 6.3 %gather_fusion = bf16[32,128,128]{2,1,0:T(8,128)(2,1)} fusion(bf16[384,128,128]{2,1,0:T(8,128)(2,1)} %get-tuple-element.162, s32[1024]{0:T(1024)S(1)} %pad_clamp_fusion.3), kind=kCustom, calls=%fused_computation.clone.1 | custom fusion | bytes 2097280 | tf_op jit(solution)/shard_map/while/body/eval_jaxpr/jit(_take)/gather | solution.py:72
  374.3 1.7 copy.62
  377.4 3.0 fusion.71
  382.2 1.8 fusion.72
  385.1 2.2 fusion.73
  389.3 6.3 %gather_fusion = bf16[32,128,128]{2,1,0:T(8,128)(2,1)} fusion(bf16[384,128,128]{2,1,0:T(8,128)(2,1)} %get-tuple-element.162, s32[1024]{0:T(1024)S(1)} %pad_clamp_fusion.3), kind=kCustom, calls=%fused_computation.clone.1 | custom fusion | bytes 2097280 | tf_op jit(solution)/shard_map/while/body/eval_jaxpr/jit(_take)/gather | solution.py:72
  398.7 3.0 fusion.71
  403.5 1.8 fusion.72
  406.4 2.2 fusion.73
  410.7 6.3 %gather_fusion = bf16[32,128,128]{2,1,0:T(8,128)(2,1)} fusion(bf16[384,128,128]{2,1,0:T(8,128)(2,1)} %get-tuple-element.162, s32[1024]{0:T(1024)S(1)} %pad_clamp_fusion.3), kind=kCustom, calls=%fused_computation.clone.1 | custom fusion | bytes 2097280 | tf_op jit(solution)/shard_map/while/body/eval_jaxpr/jit(_take)/gather | solution.py:72
  420.1 3.0 fusion.71
  424.9 1.8 fusion.72
  427.8 2.2 fusion.73
  432.0 6.3 %gather_fusion = bf16[32,128,128]{2,1,0:T(8,128)(2,1)} fusion(bf16[384,128,128]{2,1,0:T(8,128)(2,1)} %get-tuple-element.162, s32[1024]{0:T(1024)S(1)} %pad_clamp_fusion.3), kind=kCustom, calls=%fused_computation.clone.1 | custom fusion | bytes 2097280 | tf_op jit(solution)/shard_map/while/body/eval_jaxpr/jit(_take)/gather | solution.py:72
  441.4 3.0 fusion.71
  446.2 1.8 fusion.72
  449.1 2.2 fusion.73
  453.4 6.3 %gather_fusion = bf16[32,128,128]{2,1,0:T(8,128)(2,1)} fusion(bf16[384,128,128]{2,1,0:T(8,128)(2,1)} %get-tuple-element.162, s32[1024]{0:T(1024)S(1)} %pad_clamp_fusion.3), kind=kCustom, calls=%fused_computation.clone.1 | custom fusion | bytes 2097280 | tf_op jit(solution)/shard_map/while/body/eval_jaxpr/jit(_take)/gather | solution.py:72
  462.8 3.0 fusion.71
  467.5 1.8 fusion.72
  470.5 2.2 fusion.73
  474.7 6.3 %gather_fusion = bf16[32,128,128]{2,1,0:T(8,128)(2,1)} fusion(bf16[384,128,128]{2,1,0:T(8,128)(2,1)} %get-tuple-element.162, s32[1024]{0:T(1024)S(1)} %pad_clamp_fusion.3), kind=kCustom, calls=%fused_computation.clone.1 | custom fusion | bytes 2097280 | tf_op jit(solution)/shard_map/while/body/eval_jaxpr/jit(_take)/gather | solution.py:72
  484.1 3.0 fusion.71
  488.9 1.8 fusion.72
  491.8 2.2 fusion.73
  496.1 6.3 %gather_fusion = bf16[32,128,128]{2,1,0:T(8,128)(2,1)} fusion(bf16[384,128,128]{2,1,0:T(8,128)(2,1)} %get-tuple-element.162, s32[1024]{0:T(1024)S(1)} %pad_clamp_fusion.3), kind=kCustom, calls=%fused_computation.clone.1 | custom fusion | bytes 2097280 | tf_op jit(solution)/shard_map/while/body/eval_jaxpr/jit(_take)/gather | solution.py:72
  505.5 3.0 fusion.71
  510.2 1.8 fusion.72
  513.2 2.2 fusion.73
  518.0 23.0 %all_to_all.48 = bf16[4,128,768]{1,2,0:T(8,128)(2,1)S(1)} all-to-all(bf16[4,128,768]{1,2,0:T(8,128)(2,1)S(1)} %copy.46), channel_id=1, replica_groups=mesh['seq'=8,'head'=4] {'head'}, dimensions={0} | all-to-all | bytes 1572864 | tf_op jit(solution)/shard_map/all_to_all | solution.py:89
  (240 shorter events, 92.3 us)
Async XLA Ops:
  6.0 9.9 %all-to-all-start.1 = ((s32[8,1,48]{2,1,0:T(1,128)}), s32[8,1,48]{2,1,0:T(1,128)S(1)}, u32[]{:S(2)}, u32[]{:S(2)}) async-start(s32[8,1,48]{2,1,0:T(1,128)} %all_to_all.37), calls=%async_computation.1 | async-start | bytes 8192 | tf_op jit(solution)/shard_map/all_to_all | solution.py:56
  16.0 75.9 %all-to-all-start = ((bf16[128,3,3072]{0,1,2:T(4,128)(2,1)}), bf16[128,3,3072]{0,1,2:T(4,128)(2,1)S(1)}, u32[]{:S(2)}, u32[]{:S(2)}) async-start(bf16[128,3,3072]{0,1,2:T(4,128)(2,1)} %copy.35), calls=%async_computation | async-start | bytes 6291456 | tf_op jit(solution)/shard_map/all_to_all | solution.py:33
  116.6 5.8 %copy-start.1 = (s32[12,4]{0,1:T(4,128)S(1)}, s32[12,4]{0,1:T(4,128)}, u32[]{:S(2)}) copy-start(s32[12,4]{0,1:T(4,128)} %param.7) | copy-start | bytes 580
  116.6 6.0 %copy-start = (bf16[12,4,128,64]{2,3,0,1:T(8,128)(2,1)S(1)}, bf16[12,4,128,64]{2,3,0,1:T(8,128)(2,1)}, u32[]{:S(2)}) copy-start(bf16[12,4,128,64]{2,3,0,1:T(8,128)(2,1)} %get-tuple-element.69) | copy-start | bytes 2359300
  116.6 143.3 %all-to-all-start.2 = ((bf16[8,48,128,128]{3,2,1,0:T(8,128)(2,1)}), bf16[8,48,128,128]{3,2,1,0:T(8,128)(2,1)}, u32[]{:S(2)}, u32[]{:S(2)}) async-start(bf16[8,48,128,128]{3,2,1,0:T(8,128)(2,1)} %broadcast_select_fusion.1), calls=%async_computation.2 | async-start | bytes 25165824 | tf_op jit(solution)/shard_map/all_to_all | solution.py:60
where the time goes:
time: 545 us; the launch traced here: 542 us
  waiting for transfers between devices  206 us (38%)
  local copies, waits for them, and re-layouts  178 us (33%)
  other arithmetic  64.3 us (12%)
  matrix products  47.5 us (9%)
  blocking collectives  23 us (4%)
  starting transfers between devices  14.8 us (3%)
  loops' own time  8.01 us (1%)
    all_to_all x1, waiting for transfers between devices, on_device(): lax.all_to_all(served, 'seq', split_axis=0, concat_axis=0, tiled=True)  136 us
    gather x24, local copies, waits for them, and re-layouts, one_group(): jnp.take(fetched, slot_part.reshape(-1), axis=0)  95.7 us
    all_to_all x1, waiting for transfers between devices, on_device(): lax.all_to_all(projected, 'head', split_axis=2, concat_axis=0, tiled=True)  69.7 us
    concatenate x12, other arithmetic, one_group(): gathered = jnp.concatenate([own_pairs[:, None], listed], axis=1)  35.8 us
    dot_general x12, matrix products, attend_rows(): jnp.einsum('rqk,rkd->rqd', attention_weights, value_rows, preferred_eleme...  26.2 us
    all_to_all x1, blocking collectives, on_device(): lax.all_to_all(laid_out, 'head', split_axis=0, concat_axis=1, tiled=True)  23 us
    sub x12, matrix products, attend_rows(): exp_scores = jnp.exp(attention_scores - row_top)  21.2 us
    reshape x12, local copies, waits for them, and re-layouts, attend_rows(): gathered[..., :head_size]  17.7 us
  transfers between devices with their start and end apart: 3, of which 2 were waited for; matrix products, arithmetic and copies ran while one was open for 2% of the time, Pallas kernels for 0%

commit v1 on v0

--- a/solution.py
+++ b/solution.py
@@ -5,6 +5,12 @@
 from jax.sharding import PartitionSpec as P
 
 NEG_FILL = -1e30
+
+
+def stacked_exchange(shard, name, split, join):
+    pieces = jnp.split(shard, lax.axis_size(name), axis=split)
+    got = lax.all_to_all(jnp.stack(pieces), name, 0, 0)
+    return jnp.concatenate(got, axis=join)
 
 
 def attend_rows(query_part, gathered, live_cols, head_size):
@@ -30,7 +36,7 @@
 def on_device(projected, key_lists, list_counts):
     seq_count = lax.axis_size("seq")
     heads_dev, blocks_dev, list_most = key_lists.shape
-    regrouped = lax.all_to_all(projected, "head", split_axis=2, concat_axis=0, tiled=True)
+    regrouped = stacked_exchange(projected, "head", 2, 0)
     block_len = regrouped.shape[0] // blocks_dev
     group_width = regrouped.shape[2]
     head_size = group_width // heads_dev

time: 545 us -> 529 us (0.971)
  waiting for transfers between devices: 206 us -> 189 us
    all_to_all x1, waiting for transfers between devices: 69.7 us -> 52.9 us  [stacked_exchange(): got = lax.all_to_all(jnp.stack(pieces), name, 0, 0)]
  transfers between devices with their start and end apart: 3 -> 3, of which waited for: 2 -> 2; matrix products, arithmetic and copies ran while one was open for 2% -> 1% of each run, Pallas kernels for 0% -> 0%
where the time goes in v1:
time: 529 us; the launch traced here: 526 us
  waiting for transfers between devices  189 us (36%)
  local copies, waits for them, and re-layouts  177 us (33%)
  other arithmetic  66 us (12%)
  matrix products  47.5 us (9%)
  blocking collectives  23 us (4%)
  starting transfers between devices  14.8 us (3%)
  loops' own time  8.01 us (2%)
    all_to_all x1, waiting for transfers between devices, on_device(): lax.all_to_all(served, 'seq', split_axis=0, concat_axis=0, tiled=True)  136 us
    gather x24, local copies, waits for them, and re-layouts, one_group(): jnp.take(fetched, slot_part.reshape(-1), axis=0)  95.7 us
    all_to_all x1, waiting for transfers between devices, stacked_exchange(): got = lax.all_to_all(jnp.stack(pieces), name, 0, 0)  52.9 us
    concatenate x12, other arithmetic, one_group(): gathered = jnp.concatenate([own_pairs[:, None], listed], axis=1)  35.8 us
    dot_general x12, matrix products, attend_rows(): jnp.einsum('rqk,rkd->rqd', attention_weights, value_rows, preferred_eleme...  26.2 us
    all_to_all x1, blocking collectives, on_device(): lax.all_to_all(laid_out, 'head', split_axis=0, concat_axis=1, tiled=True)  23 us
    sub x12, matrix products, attend_rows(): exp_scores = jnp.exp(attention_scores - row_top)  21.2 us
    reshape x12, local copies, waits for them, and re-layouts, attend_rows(): gathered[..., :head_size]  17.7 us
  transfers between devices with their start and end apart: 3, of which 2 were waited for; matrix products, arithmetic and copies ran while one was open for 1% of the time, Pallas kernels for 0%

profile of v1, /device:TPU:2, one launch (start us, length us, event | category | flops | bytes accessed | tf_op | source)
XLA Modules:
  0.0 525.9 jit_solution(17226701897337814916)
XLA Ops:
  2.4 2.9 scatter_custom_fusion
  6.0 4.3 all-to-all-start.1
  10.3 1.8 fusion.53
  13.3 1.7 pad_maximum_fusion.1
  15.0 4.9 all-to-all-start
  21.1 52.9 %all-to-all-done = bf16[4,128,3,768]{1,3,2,0:T(8,128)(2,1)} async-done(((bf16[4,128,3,768]{1,3,2,0:T(8,128)(2,1)}), bf16[4,128,3,768]{1,3,2,0:T(8,128)(2,1)}, u32[]{:S(2)}, u32[]{:S(2)}) %all-to-all-start) | async-done | bytes 2359328 | tf_op jit(solution)/shard_map/all_to_all | solution.py:12
  74.1 3.0 slice_bitcast_fusion.1
  78.1 11.3 %gather_fusion.1 = bf16[384,128,128]{2,1,0:T(8,128)(2,1)} fusion(bf16[48,128,128]{2,1,0:T(8,128)(2,1)S(1)} %bitcast.78, s32[1024]{0:T(1024)S(1)} %pad_clamp_fusion.1), kind=kCustom, calls=%fused_computation.1 | custom fusion | bytes 25167360 | tf_op jit(solution)/shard_map/jit(_take)/gather | solution.py:63
  89.5 10.8 %broadcast_select_fusion.1 = bf16[8,48,128,128]{3,2,1,0:T(8,128)(2,1)} fusion(bf16[8,48,128,128]{3,2,1,0:T(8,128)(2,1)} %bitcast.81, pred[8,48]{1,0:T(8,128)(4,1)S(1)} %compare_and_fusion.1), kind=kLoop, calls=%fused_computation.39 | loop fusion | flops 6291456 | bytes 25166208 | tf_op jit(solution)/shard_map/jit(_take)/select_n | solution.py:63
  100.2 5.7 %all-to-all-start.2 = ((bf16[8,48,128,128]{3,2,1,0:T(8,128)(2,1)}), bf16[8,48,128,128]{3,2,1,0:T(8,128)(2,1)}, u32[]{:S(2)}, u32[]{:S(2)}) async-start(bf16[8,48,128,128]{3,2,1,0:T(8,128)(2,1)} %broadcast_select_fusion.1), calls=%async_computation.2 | async-start | bytes 25165824 | tf_op jit(solution)/shard_map/all_to_all | solution.py:66
  107.3 136.3 %all-to-all-done.2 = bf16[8,48,128,128]{3,2,1,0:T(8,128)(2,1)} async-done(((bf16[8,48,128,128]{3,2,1,0:T(8,128)(2,1)}), bf16[8,48,128,128]{3,2,1,0:T(8,128)(2,1)}, u32[]{:S(2)}, u32[]{:S(2)}) %all-to-all-start.2) | async-done | bytes 12582944 | tf_op jit(solution)/shard_map/all_to_all | solution.py:66
  243.6 256.2 %while.10 = (s32[]{:T(128)}, bf16[12,4,128,64]{2,1,3,0:T(4,128)(2,1)}, s32[12]{0:T(128)S(1)}, s32[48]{0:T(128)S(1)}, bf16[48,128,64]{1,2,0:T(8,128)(2,1)}, /*ind...) while((s32[]{:T(128)}, ...), condition=%wide.region_7.8_spmd, body=%wide.region_4.7_spmd.sunk | while | flops 234721344 | bytes 13664708 | solution.py:91
  244.9 6.3 %gather_fusion = bf16[32,128,128]{2,1,0:T(8,128)(2,1)} fusion(bf16[384,128,128]{2,1,0:T(8,128)(2,1)} %get-tuple-element.167, s32[1024]{0:T(1024)S(1)} %pad_clamp_fusion.3), kind=kCustom, calls=%fused_computation.clone.1 | custom fusion | bytes 2097280 | tf_op jit(solution)/shard_map/while/body/eval_jaxpr/jit(_take)/gather | solution.py:78
  251.2 1.7 copy.75
  254.3 3.0 fusion.72
  259.1 1.8 fusion.73
  262.0 2.2 fusion.74
  266.3 6.3 %gather_fusion = bf16[32,128,128]{2,1,0:T(8,128)(2,1)} fusion(bf16[384,128,128]{2,1,0:T(8,128)(2,1)} %get-tuple-element.167, s32[1024]{0:T(1024)S(1)} %pad_clamp_fusion.3), kind=kCustom, calls=%fused_computation.clone.1 | custom fusion | bytes 2097280 | tf_op jit(solution)/shard_map/while/body/eval_jaxpr/jit(_take)/gather | solution.py:78
  272.6 1.7 copy.75
  275.7 3.0 fusion.72
  280.4 1.8 fusion.73
  283.4 2.2 fusion.74
  287.6 6.3 %gather_fusion = bf16[32,128,128]{2,1,0:T(8,128)(2,1)} fusion(bf16[384,128,128]{2,1,0:T(8,128)(2,1)} %get-tuple-element.167, s32[1024]{0:T(1024)S(1)} %pad_clamp_fusion.3), kind=kCustom, calls=%fused_computation.clone.1 | custom fusion | bytes 2097280 | tf_op jit(solution)/shard_map/while/body/eval_jaxpr/jit(_take)/gather | solution.py:78
  293.9 1.7 copy.75
  297.0 3.0 fusion.72
  301.8 1.8 fusion.73
  304.7 2.2 fusion.74
  309.0 6.3 %gather_fusion = bf16[32,128,128]{2,1,0:T(8,128)(2,1)} fusion(bf16[384,128,128]{2,1,0:T(8,128)(2,1)} %get-tuple-element.167, s32[1024]{0:T(1024)S(1)} %pad_clamp_fusion.3), kind=kCustom, calls=%fused_computation.clone.1 | custom fusion | bytes 2097280 | tf_op jit(solution)/shard_map/while/body/eval_jaxpr/jit(_take)/gather | solution.py:78
  318.4 3.0 fusion.72
  323.1 1.8 fusion.73
  326.1 2.2 fusion.74
  330.3 6.3 %gather_fusion = bf16[32,128,128]{2,1,0:T(8,128)(2,1)} fusion(bf16[384,128,128]{2,1,0:T(8,128)(2,1)} %get-tuple-element.167, s32[1024]{0:T(1024)S(1)} %pad_clamp_fusion.3), kind=kCustom, calls=%fused_computation.clone.1 | custom fusion | bytes 2097280 | tf_op jit(solution)/shard_map/while/body/eval_jaxpr/jit(_take)/gather | solution.py:78
  339.7 3.0 fusion.72
  344.5 1.8 fusion.73
  347.4 2.2 fusion.74
  351.7 6.3 %gather_fusion = bf16[32,128,128]{2,1,0:T(8,128)(2,1)} fusion(bf16[384,128,128]{2,1,0:T(8,128)(2,1)} %get-tuple-element.167, s32[1024]{0:T(1024)S(1)} %pad_clamp_fusion.3), kind=kCustom, calls=%fused_computation.clone.1 | custom fusion | bytes 2097280 | tf_op jit(solution)/shard_map/while/body/eval_jaxpr/jit(_take)/gather | solution.py:78
  361.0 3.0 fusion.72
  365.8 1.8 fusion.73
  368.8 2.2 fusion.74
  373.0 6.3 %gather_fusion = bf16[32,128,128]{2,1,0:T(8,128)(2,1)} fusion(bf16[384,128,128]{2,1,0:T(8,128)(2,1)} %get-tuple-element.167, s32[1024]{0:T(1024)S(1)} %pad_clamp_fusion.3), kind=kCustom, calls=%fused_computation.clone.1 | custom fusion | bytes 2097280 | tf_op jit(solution)/shard_map/while/body/eval_jaxpr/jit(_take)/gather | solution.py:78
  382.4 3.0 fusion.72
  387.2 1.8 fusion.73
  390.1 2.2 fusion.74
  394.4 6.3 %gather_fusion = bf16[32,128,128]{2,1,0:T(8,128)(2,1)} fusion(bf16[384,128,128]{2,1,0:T(8,128)(2,1)} %get-tuple-element.167, s32[1024]{0:T(1024)S(1)} %pad_clamp_fusion.3), kind=kCustom, calls=%fused_computation.clone.1 | custom fusion | bytes 2097280 | tf_op jit(solution)/shard_map/while/body/eval_jaxpr/jit(_take)/gather | solution.py:78
  403.7 3.0 fusion.72
  408.5 1.8 fusion.73
  411.5 2.2 fusion.74
  415.7 6.3 %gather_fusion = bf16[32,128,128]{2,1,0:T(8,128)(2,1)} fusion(bf16[384,128,128]{2,1,0:T(8,128)(2,1)} %get-tuple-element.167, s32[1024]{0:T(1024)S(1)} %pad_clamp_fusion.3), kind=kCustom, calls=%fused_computation.clone.1 | custom fusion | bytes 2097280 | tf_op jit(solution)/shard_map/while/body/eval_jaxpr/jit(_take)/gather | solution.py:78
  425.1 3.0 fusion.72
  429.9 1.8 fusion.73
  432.8 2.2 fusion.74
  437.1 6.3 %gather_fusion = bf16[32,128,128]{2,1,0:T(8,128)(2,1)} fusion(bf16[384,128,128]{2,1,0:T(8,128)(2,1)} %get-tuple-element.167, s32[1024]{0:T(1024)S(1)} %pad_clamp_fusion.3), kind=kCustom, calls=%fused_computation.clone.1 | custom fusion | bytes 2097280 | tf_op jit(solution)/shard_map/while/body/eval_jaxpr/jit(_take)/gather | solution.py:78
  446.4 3.0 fusion.72
  451.2 1.8 fusion.73
  454.2 2.2 fusion.74
  458.4 6.3 %gather_fusion = bf16[32,128,128]{2,1,0:T(8,128)(2,1)} fusion(bf16[384,128,128]{2,1,0:T(8,128)(2,1)} %get-tuple-element.167, s32[1024]{0:T(1024)S(1)} %pad_clamp_fusion.3), kind=kCustom, calls=%fused_computation.clone.1 | custom fusion | bytes 2097280 | tf_op jit(solution)/shard_map/while/body/eval_jaxpr/jit(_take)/gather | solution.py:78
  467.8 3.0 fusion.72
  472.6 1.8 fusion.73
  475.5 2.2 fusion.74
  479.7 6.3 %gather_fusion = bf16[32,128,128]{2,1,0:T(8,128)(2,1)} fusion(bf16[384,128,128]{2,1,0:T(8,128)(2,1)} %get-tuple-element.167, s32[1024]{0:T(1024)S(1)} %pad_clamp_fusion.3), kind=kCustom, calls=%fused_computation.clone.1 | custom fusion | bytes 2097280 | tf_op jit(solution)/shard_map/while/body/eval_jaxpr/jit(_take)/gather | solution.py:78
  489.1 3.0 fusion.72
  493.9 1.8 fusion.73
  496.9 2.2 fusion.74
  501.7 23.0 %all_to_all.38 = bf16[4,128,768]{1,2,0:T(8,128)(2,1)S(1)} all-to-all(bf16[4,128,768]{1,2,0:T(8,128)(2,1)S(1)} %copy.56), channel_id=1, replica_groups=mesh['seq'=8,'head'=4] {'head'}, dimensions={0} | all-to-all | bytes 1572864 | tf_op jit(solution)/shard_map/all_to_all | solution.py:95
  (242 shorter events, 95.2 us)
Async XLA Ops:
  6.0 8.9 %all-to-all-start.1 = ((s32[8,1,48]{2,1,0:T(1,128)}), s32[8,1,48]{2,1,0:T(1,128)S(1)}, u32[]{:S(2)}, u32[]{:S(2)}) async-start(s32[8,1,48]{2,1,0:T(1,128)} %all_to_all.27), calls=%async_computation.1 | async-start | bytes 8192 | tf_op jit(solution)/shard_map/all_to_all | solution.py:62
  15.0 59.1 %all-to-all-start = ((bf16[4,128,3,768]{1,3,2,0:T(8,128)(2,1)}), bf16[4,128,3,768]{1,3,2,0:T(8,128)(2,1)}, u32[]{:S(2)}, u32[]{:S(2)}) async-start(bf16[4,128,3,768]{1,3,2,0:T(8,128)(2,1)} %pad_maximum_fusion.1), calls=%async_computation | async-start | bytes 4718592 | tf_op jit(solution)/shard_map/all_to_all | solution.py:12
  100.2 5.8 %copy-start.1 = (s32[12,4]{0,1:T(4,128)S(1)}, s32[12,4]{0,1:T(4,128)}, u32[]{:S(2)}) copy-start(s32[12,4]{0,1:T(4,128)} %param.7) | copy-start | bytes 580
  100.2 6.0 %copy-start = (bf16[12,4,128,64]{2,3,0,1:T(8,128)(2,1)S(1)}, bf16[12,4,128,64]{2,3,0,1:T(8,128)(2,1)}, u32[]{:S(2)}) copy-start(bf16[12,4,128,64]{2,3,0,1:T(8,128)(2,1)} %get-tuple-element.70) | copy-start | bytes 2359300
  100.2 143.3 %all-to-all-start.2 = ((bf16[8,48,128,128]{3,2,1,0:T(8,128)(2,1)}), bf16[8,48,128,128]{3,2,1,0:T(8,128)(2,1)}, u32[]{:S(2)}, u32[]{:S(2)}) async-start(bf16[8,48,128,128]{3,2,1,0:T(8,128)(2,1)} %broadcast_select_fusion.1), calls=%async_computation.2 | async-start | bytes 25165824 | tf_op jit(solution)/shard_map/all_to_all | solution.py:66
